TPU v7x, 256 devices: a whole 4x4x8 slice. The times are simulated.
256 devices in a mesh: dp: 16 (over y, x), seq: 16 (over z, core).
Axes of the slice: x: 4, y: 4, z: 8, core: 2. Of those that a mesh axis runs over, the one named last changes fastest.
Arguments:
- query_proj: bfloat16 [16, 3072, 1024], P('dp', 'seq'), may hold values from -6 to 6
- key_proj: bfloat16 [16, 3072, 1024], P('dp', 'seq'), may hold values from -6 to 6
- value_proj: bfloat16 [16, 3072, 1024], P('dp', 'seq'), may hold values from -6 to 6
- cotangent: bfloat16 [16, 3072, 1024], P('dp', 'seq'), may hold values from -6 to 6
- out_weight: bfloat16 [1024, 1024], replicated, may hold values from -0.1875 to 0.1875
- conv_weight: float32 [31, 1024], replicated, may hold values from -1 to 1
- rec_starts: int32 [16, 2], P('dp'), may hold values from 0 to 3064, as said below
Outputs:
- layer_out: bfloat16 [16, 3072, 1024], P('dp', 'seq')
- query_grad: bfloat16 [16, 3072, 1024], P('dp', 'seq')
- key_grad: bfloat16 [16, 3072, 1024], P('dp', 'seq')
- value_grad: bfloat16 [16, 3072, 1024], P('dp', 'seq')
- weight_grad: float32 [1024, 1024], replicated
- conv_grad: float32 [31, 1024], replicated
Inputs may be any that keep to these rules, and one draw needn't show every extreme that they name: `rec_starts`: in each group the first start is 0, the starts rise strictly and each is a multiple of 8; a recording runs up to the next start, the last one to frame 3072 - 1.
All inputs are finite; a program needn't handle non-finite values.
Results may differ from a plain program's by a relative error of at most 0.02.
Values may be sent and summed in bfloat16 or wider, within the bound.
A program may use at most 64 MiB of HBM per device.

v0:
```python
import math
import jax
import jax.numpy as jnp
from jax import lax
from jax.sharding import PartitionSpec as P

HEAD_DIM = 64
KERN = 31
LAG = 30


def shifted(value, axis, steps):
    count = lax.axis_size(axis)
    leading, last = (max(0, -steps), min(count, count - steps))
    return lax.ppermute(value, axis, [(source, source + steps) for source in range(leading, last)])


def record_ids(frames, starts_row, total):
    above = (frames[:, None] >= starts_row[None, :]).astype(jnp.int32)
    labels = jnp.sum(above, axis=1) - 1
    inside = (frames >= 0) & (frames < total)
    return jnp.where(inside, labels, -2)


def depthwise(padded, labels_pad, labels_out, weights, count):
    total = jnp.zeros((count, padded.shape[1]), jnp.float32)
    for tap in range(weights.shape[0]):
        window = padded[tap : tap + count].astype(jnp.float32)
        same = (labels_pad[tap : tap + count] == labels_out)[:, None]
        total = total + jnp.where(same, weights[tap][None, :] * window, 0.0)
    return total


def transposed(padded, labels_pad, labels_out, weights, count):
    total = jnp.zeros((count, padded.shape[1]), jnp.float32)
    last = weights.shape[0] - 1
    for tap in range(weights.shape[0]):
        offset = last - tap
        window = padded[offset : offset + count].astype(jnp.float32)
        same = (labels_pad[offset : offset + count] == labels_out)[:, None]
        total = total + jnp.where(same, weights[tap][None, :] * window, 0.0)
    return total


def tap_sums(signal, padded, labels_pad, labels_out, taps):
    count = signal.shape[0]
    rows_out = []
    for tap in range(taps):
        window = padded[tap : tap + count].astype(jnp.float32)
        same = (labels_pad[tap : tap + count] == labels_out)[:, None]
        rows_out.append(jnp.sum(jnp.where(same, signal * window, 0.0), axis=0))
    return jnp.stack(rows_out)


def silu_parts(conv):
    gate_value = jax.nn.sigmoid(conv)
    return (conv * gate_value, gate_value * (1.0 + conv * (1.0 - gate_value)))


def block_scores(query_blk, key_part, labels_q, labels_k, scale):
    raw = (
        jnp.einsum("qhd,khd->hqk", query_blk, key_part, preferred_element_type=jnp.float32) * scale
    )
    same = (labels_q[:, None] == labels_k[None, :])[None]
    return jnp.where(same, raw, -1e30)


def block_grads(
    query_blk, key_part, value_part, mixed_blk, back_blk, labels_q, labels_k, norm_blk, scale
):
    scores = block_scores(query_blk, key_part, labels_q, labels_k, scale)
    probs = jnp.exp(scores - norm_blk[:, :, None]).astype(jnp.bfloat16)
    prob_back = jnp.einsum("qhd,khd->hqk", back_blk, value_part, preferred_element_type=jnp.float32)
    delta = jnp.sum(back_blk.astype(jnp.float32) * mixed_blk.astype(jnp.float32), axis=2).T
    score_back = (probs.astype(jnp.float32) * (prob_back - delta[:, :, None])).astype(jnp.bfloat16)
    return (probs, score_back)


def forward_dense(heads_q, heads_k, heads_v, labels, width, scale):
    total, heads_here, features = heads_q.shape
    count = total // width

    def forward_one_block(index):
        start = index * width
        query_blk = lax.dynamic_slice_in_dim(heads_q, start, width, 0)
        labels_q = lax.dynamic_slice_in_dim(labels, start, width, 0)
        scores = block_scores(query_blk, heads_k, labels_q, labels, scale)
        top = jnp.max(scores, axis=2, keepdims=True)
        norm = top + jnp.log(jnp.sum(jnp.exp(scores - top), axis=2, keepdims=True))
        probs = jnp.exp(scores - norm).astype(jnp.bfloat16)
        mixed_blk = jnp.einsum("hqk,khd->qhd", probs, heads_v, preferred_element_type=jnp.float32)
        return (mixed_blk.astype(jnp.bfloat16), norm[:, :, 0])

    mixed_blocks, norm_blocks = lax.map(forward_one_block, jnp.arange(count, dtype=jnp.int32))
    mixed_heads = mixed_blocks.reshape(total, heads_here, features)
    norms = norm_blocks.transpose(1, 0, 2).reshape(heads_here, total)
    return (mixed_heads, norms)


def backward_dense(heads_q, heads_k, heads_v, mixed_heads, back_heads, norms, labels, width, scale):
    total = heads_q.shape[0]
    count = total // width
    empty = jnp.zeros(heads_k.shape, jnp.float32)

    def backward_one_block(carry, index):
        key_acc, value_acc = carry
        start = index * width
        query_blk = lax.dynamic_slice_in_dim(heads_q, start, width, 0)
        mixed_blk = lax.dynamic_slice_in_dim(mixed_heads, start, width, 0)
        back_blk = lax.dynamic_slice_in_dim(back_heads, start, width, 0)
        labels_q = lax.dynamic_slice_in_dim(labels, start, width, 0)
        norm_blk = lax.dynamic_slice_in_dim(norms, start, width, 1)
        probs, score_back = block_grads(
            query_blk, heads_k, heads_v, mixed_blk, back_blk, labels_q, labels, norm_blk, scale
        )
        query_part = scale * jnp.einsum(
            "hqk,khd->qhd", score_back, heads_k, preferred_element_type=jnp.float32
        )
        key_acc = key_acc + scale * jnp.einsum(
            "hqk,qhd->khd", score_back, query_blk, preferred_element_type=jnp.float32
        )
        value_acc = value_acc + jnp.einsum(
            "hqk,qhd->khd", probs, back_blk, preferred_element_type=jnp.float32
        )
        return ((key_acc, value_acc), query_part.astype(jnp.bfloat16))

    sums, query_blocks = lax.scan(
        backward_one_block, (empty, empty), jnp.arange(count, dtype=jnp.int32)
    )
    query_grads = query_blocks.reshape(heads_q.shape)
    return (query_grads, sums[0].astype(jnp.bfloat16), sums[1].astype(jnp.bfloat16))


def local(query_proj, key_proj, value_proj, cotangent, out_weight, conv_weight, rec_starts):
    rows = query_proj.shape[1]
    parts = lax.axis_size("seq")
    place = lax.axis_index("seq")
    total = rows * parts
    width = min(512, total)
    scale = HEAD_DIM ** (-0.5)
    starts_row = rec_starts[0]
    sent = (
        lax.all_to_all(query_proj[0], "seq", split_axis=1, concat_axis=0, tiled=True),
        lax.all_to_all(key_proj[0], "seq", split_axis=1, concat_axis=0, tiled=True),
        lax.all_to_all(value_proj[0], "seq", split_axis=1, concat_axis=0, tiled=True),
    )
    heads_q = sent[0].reshape(total, -1, HEAD_DIM)
    heads_k = sent[1].reshape(total, -1, HEAD_DIM)
    heads_v = sent[2].reshape(total, -1, HEAD_DIM)
    labels = record_ids(jnp.arange(total, dtype=jnp.int32), starts_row, total)
    mixed_heads, norms = forward_dense(heads_q, heads_k, heads_v, labels, width, scale)
    mixed_rows = lax.all_to_all(
        mixed_heads.reshape(total, -1), "seq", split_axis=0, concat_axis=1, tiled=True
    )
    projected = jnp.dot(mixed_rows, out_weight, preferred_element_type=jnp.float32).astype(
        jnp.bfloat16
    )
    labels_local = record_ids(place * rows + jnp.arange(rows, dtype=jnp.int32), starts_row, total)
    cot = cotangent[0]
    behind = shifted(projected[rows - LAG :], "seq", 1)
    padded = jnp.concatenate([behind, projected], axis=0)
    labels_pad = record_ids(
        place * rows - LAG + jnp.arange(rows + LAG, dtype=jnp.int32), starts_row, total
    )
    labels_back = record_ids(
        place * rows + jnp.arange(rows + LAG, dtype=jnp.int32), starts_row, total
    )
    conv = depthwise(padded, labels_pad, labels_local, conv_weight, rows)
    activated, slope = silu_parts(conv)
    conv_back = cot.astype(jnp.float32) * slope
    ahead_back = shifted(conv_back[:LAG].astype(jnp.bfloat16), "seq", -1).astype(jnp.float32)
    back_pad = jnp.concatenate([conv_back, ahead_back], axis=0)
    layer_out = (projected.astype(jnp.float32) + activated).astype(jnp.bfloat16)
    spread = transposed(back_pad, labels_back, labels_local, conv_weight, rows)
    proj_back = (cot.astype(jnp.float32) + spread).astype(jnp.bfloat16)
    conv_local = tap_sums(conv_back, padded, labels_pad, labels_local, KERN)
    factor = 1.0 / math.sqrt(lax.axis_size("dp") * total)
    weight_local = lax.dot_general(
        mixed_rows, proj_back, (((0,), (0,)), ((), ())), preferred_element_type=jnp.float32
    )
    summed = lax.psum((weight_local, conv_local), ("dp", "seq"))
    weight_grad = summed[0] * factor
    conv_grad = summed[1] * factor
    mixed_back = lax.dot_general(
        proj_back, out_weight, (((1,), (1,)), ((), ())), preferred_element_type=jnp.float32
    ).astype(jnp.bfloat16)
    back_heads = lax.all_to_all(mixed_back, "seq", split_axis=1, concat_axis=0, tiled=True).reshape(
        total, -1, HEAD_DIM
    )
    grad_q, grad_k, grad_v = backward_dense(
        heads_q, heads_k, heads_v, mixed_heads, back_heads, norms, labels, width, scale
    )
    returned = (
        lax.all_to_all(grad_q.reshape(total, -1), "seq", split_axis=0, concat_axis=1, tiled=True),
        lax.all_to_all(grad_k.reshape(total, -1), "seq", split_axis=0, concat_axis=1, tiled=True),
        lax.all_to_all(grad_v.reshape(total, -1), "seq", split_axis=0, concat_axis=1, tiled=True),
    )
    return (
        layer_out[None],
        returned[0][None],
        returned[1][None],
        returned[2][None],
        weight_grad,
        conv_grad,
    )


def solution(mesh):
    return jax.shard_map(
        local,
        mesh=mesh,
        in_specs=(
            P("dp", "seq", None),
            P("dp", "seq", None),
            P("dp", "seq", None),
            P("dp", "seq", None),
            P(),
            P(),
            P("dp", None),
        ),
        out_specs=(
            P("dp", "seq", None),
            P("dp", "seq", None),
            P("dp", "seq", None),
            P("dp", "seq", None),
            P(),
            P(),
        ),
        check_vma=False,
    )
```

profile of v0, /device:TPU:2, one launch (start us, length us, event | category | flops | bytes accessed | tf_op | source)
XLA Modules:
  0.0 611.4 jit_solution(17486042419321726274)
XLA Ops:
  9.3 8.6 %all-to-all-start = ((bf16[192,16,64]{0,2,1:T(8,128)(2,1)}), bf16[192,16,64]{0,2,1:T(8,128)(2,1)S(1)}, u32[]{:S(2)}, u32[]{:S(2)}) async-start(bf16[192,16,64]{0,2,1:T(8,128)(2,1)} %bitcast.10), calls=%async_computation | async-start | bytes 1048576 | tf_op jit(solution)/shard_map/all_to_all | solution.py:143
  21.9 12.0 %all-to-all-done = bf16[192,16,64]{0,2,1:T(8,128)(2,1)S(1)} async-done(((bf16[192,16,64]{0,2,1:T(8,128)(2,1)}), bf16[192,16,64]{0,2,1:T(8,128)(2,1)S(1)}, u32[]{:S(2)}, u32[]{:S(2)}) %all-to-all-start) | async-done | bytes 393248 | tf_op jit(solution)/shard_map/all_to_all | solution.py:143
  33.9 4.2 all-to-all-start.1
  39.7 14.6 %all-to-all-done.1 = bf16[192,16,64]{0,2,1:T(8,128)(2,1)S(1)} async-done(((bf16[192,16,64]{0,2,1:T(8,128)(2,1)}), bf16[192,16,64]{0,2,1:T(8,128)(2,1)S(1)}, u32[]{:S(2)}, u32[]{:S(2)}) %all-to-all-start.1) | async-done | bytes 393248 | tf_op jit(solution)/shard_map/all_to_all | solution.py:144
  54.3 4.2 all-to-all-start.2
  64.1 10.5 %all-to-all-done.2 = bf16[192,16,64]{0,2,1:T(8,128)(2,1)} async-done(((bf16[192,16,64]{0,2,1:T(8,128)(2,1)}), bf16[192,16,64]{0,2,1:T(8,128)(2,1)}, u32[]{:S(2)}, u32[]{:S(2)}) %all-to-all-start.2) | async-done | bytes 393248 | tf_op jit(solution)/shard_map/all_to_all | solution.py:145
  76.5 37.1 %while.27 = (s32[]{:T(128)}, bf16[6,512,1,64]{1,3,2,0:T(8,128)(2,1)S(1)}, f32[6,1,512]{2,1,0:T(1,128)}, s32[6]{0:T(128)S(1)}, s32[3072]{0:T(1024)S(1)}, /*index=...) while((s32[]{:T(128)}, ...), condition=%wide.region_4.5_spmd, body=%wide.region_1.4_spmd.sunk | while | flops 415268352 | bytes 19828936 | solution.py:94
  119.2 4.1 all-to-all-start.3
  128.5 11.0 %all-to-all-done.3 = bf16[16,192,64]{1,2,0:T(8,128)(2,1)S(1)} async-done(((bf16[16,192,64]{1,2,0:T(8,128)(2,1)}), bf16[16,192,64]{1,2,0:T(8,128)(2,1)S(1)}, u32[]{:S(2)}, u32[]{:S(2)}) %all-to-all-start.3) | async-done | bytes 393248 | tf_op jit(solution)/shard_map/all_to_all | solution.py:152
  140.8 3.6 collective-permute-start
  148.1 19.4 %fusion.155 = (f32[1024]{0:T(1024)S(1)}, f32[192,1024]{1,0:T(8,128)S(1)}, f32[192,1024]{1,0:T(8,128)}) fusion(bf16[192,1024]{1,0:T(8,128)(2,1)} %copy-done.1, pred[192]{0:T(512)(128)(4,1)} %get-tuple-element.318, bf16[1,192,1024]{2,1,0:T(8,128)(2,1)} %param.14, f32[1024]{0:T(1024)} %bitcast.257, bf16[30,1024]{1,0:T(8,128)(2,1)S(1)} %collective-permute-done, ...), kind=kLoop, calls=%fused_computation.322 | loop fusion | flops 44235776 | bytes 2557760 | tf_op jit(solution)/shard_map/reduce_sum | solution.py:51
  168.8 3.9 fusion.90
  172.8 4.0 fusion.108
  179.8 9.1 %fusion.151 = bf16[192,1024]{1,0:T(8,128)(2,1)S(1)} fusion(f32[192,1024]{1,0:T(8,128)S(1)} %get-tuple-element.250, f32[30,1024]{1,0:T(8,128)S(1)} %convert_element_type.251, bf16[1,192,1024]{2,1,0:T(8,128)(2,1)S(1)} %copy-done.15, f32[1024]{0:T(1024)S(1)} %bitcast.258, f32[1024]{0:T(1024)S(1)} %bitcast.260, f32[1024]{0:T(1024)S(1)} %bitcast.264, ...), kind=kLoop, calls=%fused_computation.318 | loop fusion | flops 24576000 | bytes 1828672 | tf_op jit(solution)/shard_map/convert_element_type | solution.py:175
  193.4 6.2 %all-to-all-start.4 = ((bf16[192,16,64]{0,2,1:T(8,128)(2,1)}), bf16[192,16,64]{0,2,1:T(8,128)(2,1)}, u32[]{:S(2)}, u32[]{:S(2)}) async-start(bf16[192,16,64]{0,2,1:T(8,128)(2,1)} %bitcast.230), calls=%async_computation.4 | async-start | bytes 1048576 | tf_op jit(solution)/shard_map/all_to_all | solution.py:187
  199.5 4.1 fusion.150
  203.7 4.2 fusion.126
  210.5 5.1 all-to-all-done.4
  219.0 82.6 %while.28 = (s32[]{:T(128)}, f32[3072,1,64]{0,2,1:T(8,128)}, f32[3072,1,64]{0,2,1:T(8,128)}, bf16[6,512,1,64]{1,3,2,0:T(8,128)(2,1)}, s32[6]{0:T(128)S(1)}, /*in...) while((s32[]{:T(128)}, f32[3072,1,64]{0,2,1:T(8,128)}, ...), condition=%wide.region_10.11_spmd.clone, body=%wide.region_8.10_spmd.clone.sunk | while | flops 1021967872 | bytes 37843340 | solution.py:127
  222.1 2.7 exponential_convert_fusion.12
  235.8 2.8 exponential_convert_fusion.12
  263.3 2.7 exponential_convert_fusion.12
  277.1 2.8 exponential_convert_fusion.12
  304.4 4.2 all-to-all-start.5
  308.7 3.9 fusion.313
  319.1 5.8 all-to-all-done.5
  324.8 4.2 all-to-all-start.6
  332.5 15.0 %all-to-all-done.6 = bf16[16,192,64]{1,2,0:T(8,128)(2,1)} async-done(((bf16[16,192,64]{1,2,0:T(8,128)(2,1)}), bf16[16,192,64]{1,2,0:T(8,128)(2,1)}, u32[]{:S(2)}, u32[]{:S(2)}) %all-to-all-start.6) | async-done | bytes 393248 | tf_op jit(solution)/shard_map/all_to_all | solution.py:195
  347.5 3.8 all-to-all-start.7
  357.4 11.8 %all-to-all-done.7 = bf16[16,192,64]{1,2,0:T(8,128)(2,1)S(1)} async-done(((bf16[16,192,64]{1,2,0:T(8,128)(2,1)}), bf16[16,192,64]{1,2,0:T(8,128)(2,1)S(1)}, u32[]{:S(2)}, u32[]{:S(2)}) %all-to-all-start.7) | async-done | bytes 393248 | tf_op jit(solution)/shard_map/all_to_all | solution.py:196
  370.2 228.6 %all-reduce.3.cloned.1.call-done = (f32[1024,1024]{1,0:T(8,128)}, f32[31,1024]{1,0:T(8,128)}) async-done(((f32[1024,1024]{1,0:T(8,128)}, f32[31,1024]{1,0:T(8,128)}), (f32[1024,1024]{1,0:T(8,128)}, f32[31,1024]{1,0:T(8,128)})) %all-reduce.3.cloned.1.call-update) | async-done | bytes 4321296 | tf_op jit(solution)/shard_map/psum | solution.py:181
  598.8 5.2 broadcast_multiply_fusion
  (324 shorter events, 165.3 us)
Async XLA Ops:
  7.2 132.3 %copy-start = (bf16[1024,1024]{1,0:T(8,128)(2,1)S(1)}, bf16[1024,1024]{1,0:T(8,128)(2,1)}, u32[]{:S(2)}) copy-start(bf16[1024,1024]{1,0:T(8,128)(2,1)} %param.15) | copy-start | bytes 6291460
  9.3 24.6 %all-to-all-start = ((bf16[192,16,64]{0,2,1:T(8,128)(2,1)}), bf16[192,16,64]{0,2,1:T(8,128)(2,1)S(1)}, u32[]{:S(2)}, u32[]{:S(2)}) async-start(bf16[192,16,64]{0,2,1:T(8,128)(2,1)} %bitcast.10), calls=%async_computation | async-start | bytes 1048576 | tf_op jit(solution)/shard_map/all_to_all | solution.py:143
  33.9 20.4 %all-to-all-start.1 = ((bf16[192,16,64]{0,2,1:T(8,128)(2,1)}), bf16[192,16,64]{0,2,1:T(8,128)(2,1)S(1)}, u32[]{:S(2)}, u32[]{:S(2)}) async-start(bf16[192,16,64]{0,2,1:T(8,128)(2,1)} %bitcast.12), calls=%async_computation.1 | async-start | bytes 1048576 | tf_op jit(solution)/shard_map/all_to_all | solution.py:144
  54.3 20.3 %all-to-all-start.2 = ((bf16[192,16,64]{0,2,1:T(8,128)(2,1)}), bf16[192,16,64]{0,2,1:T(8,128)(2,1)}, u32[]{:S(2)}, u32[]{:S(2)}) async-start(bf16[192,16,64]{0,2,1:T(8,128)(2,1)} %bitcast.14), calls=%async_computation.2 | async-start | bytes 1048576 | tf_op jit(solution)/shard_map/all_to_all | solution.py:145
  59.9 64.1 %copy-start.48 = (s32[192]{0:T(256)}, s32[192]{0:T(256)S(1)}, u32[]{:S(2)}) copy-start(s32[192]{0:T(256)S(1)} %get-tuple-element.253) | copy-start | bytes 2308
  113.6 34.4 %copy-start.9 = (bf16[3072,1,64]{0,2,1:T(8,128)(2,1)}, bf16[3072,1,64]{0,2,1:T(8,128)(2,1)S(1)}, u32[]{:S(2)}) copy-start(bf16[3072,1,64]{0,2,1:T(8,128)(2,1)S(1)} %get-tuple-element.567) | copy-start | bytes 1179652
  119.2 20.3 %all-to-all-start.3 = ((bf16[16,192,64]{1,2,0:T(8,128)(2,1)}), bf16[16,192,64]{1,2,0:T(8,128)(2,1)S(1)}, u32[]{:S(2)}, u32[]{:S(2)}) async-start(bf16[16,192,64]{1,2,0:T(8,128)(2,1)} %copy.63), calls=%async_computation.3 | async-start | bytes 1048576 | tf_op jit(solution)/shard_map/all_to_all | solution.py:152
  140.8 7.2 %collective-permute-start = (bf16[30,1024]{1,0:T(8,128)(2,1)S(1)}, bf16[30,1024]{1,0:T(8,128)(2,1)S(1)}, u32[]{:S(2)}, u32[]{:S(2)}) collective-permute-start(bf16[30,1024]{1,0:T(8,128)(2,1)S(1)} %slice.713), channel_id=1, source_target_pairs={{0,1},{1,2},{2,3},{3,4},{4,5},{5,6},{6,7},{7,8},{8,9},{9,10},{10,1... | collective-permute-start | bytes 184328 | tf_op jit(solution)/shard_map/ppermute | solution.py:15
  145.8 33.7 %copy-start.17 = (f32[1,1024]{1,0:T(1,128)S(1)}, f32[1,1024]{1,0:T(1,128)}, u32[]{:S(2)}) copy-start(f32[1,1024]{1,0:T(1,128)} %get-tuple-element.275) | copy-start | bytes 12292
  145.8 33.6 %copy-start.15 = (bf16[1,192,1024]{2,1,0:T(8,128)(2,1)S(1)}, bf16[1,192,1024]{2,1,0:T(8,128)(2,1)}, u32[]{:S(2)}) copy-start(bf16[1,192,1024]{2,1,0:T(8,128)(2,1)} %param.14) | copy-start | bytes 1179652
  145.8 33.6 %copy-start.18 = (f32[1,1024]{1,0:T(1,128)S(1)}, f32[1,1024]{1,0:T(1,128)}, u32[]{:S(2)}) copy-start(f32[1,1024]{1,0:T(1,128)} %get-tuple-element.276) | copy-start | bytes 12292
  145.8 33.6 %copy-start.19 = (f32[1,1024]{1,0:T(1,128)S(1)}, f32[1,1024]{1,0:T(1,128)}, u32[]{:S(2)}) copy-start(f32[1,1024]{1,0:T(1,128)} %get-tuple-element.277) | copy-start | bytes 12292
  145.9 33.6 %copy-start.20 = (f32[1,1024]{1,0:T(1,128)S(1)}, f32[1,1024]{1,0:T(1,128)}, u32[]{:S(2)}) copy-start(f32[1,1024]{1,0:T(1,128)} %get-tuple-element.278) | copy-start | bytes 12292
  145.9 33.6 %copy-start.21 = (f32[1,1024]{1,0:T(1,128)S(1)}, f32[1,1024]{1,0:T(1,128)}, u32[]{:S(2)}) copy-start(f32[1,1024]{1,0:T(1,128)} %get-tuple-element.279) | copy-start | bytes 12292
  145.9 33.6 %copy-start.22 = (f32[1,1024]{1,0:T(1,128)S(1)}, f32[1,1024]{1,0:T(1,128)}, u32[]{:S(2)}) copy-start(f32[1,1024]{1,0:T(1,128)} %get-tuple-element.280) | copy-start | bytes 12292
  145.9 33.6 %copy-start.23 = (f32[1,1024]{1,0:T(1,128)S(1)}, f32[1,1024]{1,0:T(1,128)}, u32[]{:S(2)}) copy-start(f32[1,1024]{1,0:T(1,128)} %get-tuple-element.281) | copy-start | bytes 12292
  145.9 33.6 %copy-start.24 = (f32[1,1024]{1,0:T(1,128)S(1)}, f32[1,1024]{1,0:T(1,128)}, u32[]{:S(2)}) copy-start(f32[1,1024]{1,0:T(1,128)} %get-tuple-element.282) | copy-start | bytes 12292
  145.9 33.6 %copy-start.25 = (f32[1,1024]{1,0:T(1,128)S(1)}, f32[1,1024]{1,0:T(1,128)}, u32[]{:S(2)}) copy-start(f32[1,1024]{1,0:T(1,128)} %get-tuple-element.283) | copy-start | bytes 12292
  145.9 33.6 %copy-start.26 = (f32[1,1024]{1,0:T(1,128)S(1)}, f32[1,1024]{1,0:T(1,128)}, u32[]{:S(2)}) copy-start(f32[1,1024]{1,0:T(1,128)} %get-tuple-element.284) | copy-start | bytes 12292
  145.9 33.6 %copy-start.27 = (f32[1,1024]{1,0:T(1,128)S(1)}, f32[1,1024]{1,0:T(1,128)}, u32[]{:S(2)}) copy-start(f32[1,1024]{1,0:T(1,128)} %get-tuple-element.285) | copy-start | bytes 12292
  145.9 33.6 %copy-start.28 = (f32[1,1024]{1,0:T(1,128)S(1)}, f32[1,1024]{1,0:T(1,128)}, u32[]{:S(2)}) copy-start(f32[1,1024]{1,0:T(1,128)} %get-tuple-element.286) | copy-start | bytes 12292
  145.9 33.6 %copy-start.29 = (f32[1,1024]{1,0:T(1,128)S(1)}, f32[1,1024]{1,0:T(1,128)}, u32[]{:S(2)}) copy-start(f32[1,1024]{1,0:T(1,128)} %get-tuple-element.256) | copy-start | bytes 12292
  146.0 33.6 %copy-start.30 = (f32[1,1024]{1,0:T(1,128)S(1)}, f32[1,1024]{1,0:T(1,128)}, u32[]{:S(2)}) copy-start(f32[1,1024]{1,0:T(1,128)} %get-tuple-element.257) | copy-start | bytes 12292
  146.0 33.6 %copy-start.31 = (f32[1,1024]{1,0:T(1,128)S(1)}, f32[1,1024]{1,0:T(1,128)}, u32[]{:S(2)}) copy-start(f32[1,1024]{1,0:T(1,128)} %get-tuple-element.258) | copy-start | bytes 12292
  146.0 33.6 %copy-start.32 = (f32[1,1024]{1,0:T(1,128)S(1)}, f32[1,1024]{1,0:T(1,128)}, u32[]{:S(2)}) copy-start(f32[1,1024]{1,0:T(1,128)} %get-tuple-element.259) | copy-start | bytes 12292
  167.5 11.9 %collective-permute-start.1 = (bf16[30,1024]{1,0:T(8,128)(2,1)S(1)}, bf16[30,1024]{1,0:T(8,128)(2,1)S(1)}, u32[]{:S(2)}, u32[]{:S(2)}) collective-permute-start(bf16[30,1024]{1,0:T(8,128)(2,1)S(1)} %slice.1694), channel_id=1, source_target_pairs={{1,0},{2,1},{3,2},{4,3},{5,4},{6,5},{7,6},{8,7},{9,8},{10,9},{11,1... | collective-permute-start | bytes 184328 | tf_op jit(solution)/shard_map/ppermute | solution.py:15
  193.4 22.2 %all-to-all-start.4 = ((bf16[192,16,64]{0,2,1:T(8,128)(2,1)}), bf16[192,16,64]{0,2,1:T(8,128)(2,1)}, u32[]{:S(2)}, u32[]{:S(2)}) async-start(bf16[192,16,64]{0,2,1:T(8,128)(2,1)} %bitcast.230), calls=%async_computation.4 | async-start | bytes 1048576 | tf_op jit(solution)/shard_map/all_to_all | solution.py:187
  304.4 20.5 %all-to-all-start.5 = ((bf16[16,192,64]{1,2,0:T(8,128)(2,1)}), bf16[16,192,64]{1,2,0:T(8,128)(2,1)}, u32[]{:S(2)}, u32[]{:S(2)}) async-start(bf16[16,192,64]{1,2,0:T(8,128)(2,1)} %copy.68), calls=%async_computation.5 | async-start | bytes 1048576 | tf_op jit(solution)/shard_map/all_to_all | solution.py:194
  308.7 290.1 %all-reduce.3.cloned.1.call-start = ((), (), s32[]{:S(2)}) async-start(), calls=%async_computation.8 | async-start | bytes 8650752 | tf_op jit(solution)/shard_map/psum | solution.py:181
  312.6 38.7 %copy-start.3 = (bf16[192,1024]{1,0:T(8,128)(2,1)S(1)}, bf16[192,1024]{1,0:T(8,128)(2,1)}, u32[]{:S(2)}) copy-start(bf16[192,1024]{1,0:T(8,128)(2,1)} %copy-done.1) | copy-start | bytes 1179652
  324.8 22.7 %all-to-all-start.6 = ((bf16[16,192,64]{1,2,0:T(8,128)(2,1)}), bf16[16,192,64]{1,2,0:T(8,128)(2,1)}, u32[]{:S(2)}, u32[]{:S(2)}) async-start(bf16[16,192,64]{1,2,0:T(8,128)(2,1)} %copy.69), calls=%async_computation.6 | async-start | bytes 1048576 | tf_op jit(solution)/shard_map/all_to_all | solution.py:195
  347.5 21.7 %all-to-all-start.7 = ((bf16[16,192,64]{1,2,0:T(8,128)(2,1)}), bf16[16,192,64]{1,2,0:T(8,128)(2,1)S(1)}, u32[]{:S(2)}, u32[]{:S(2)}) async-start(bf16[16,192,64]{1,2,0:T(8,128)(2,1)} %copy.70), calls=%async_computation.7 | async-start | bytes 1048576 | tf_op jit(solution)/shard_map/all_to_all | solution.py:196
  (63 other events, 990.4 us)
Sparse Core Ops, SparseCore 0:
  315.6 283.1 all-reduce.2
where the time goes:
time: 615 us; the launch traced here: 611 us
  waiting for transfers between devices  314 us (51%)
  matrix products  84.2 us (14%)
  other arithmetic  76 us (12%)
  local copies, waits for them, and re-layouts  68.6 us (11%)
  starting transfers between devices  44.5 us (7%)
  between operations  15 us (2%)
  loops' own time  8.71 us (1%)
    psum x1, waiting for transfers between devices, local(): summed = lax.psum((weight_local, conv_local), ('dp', 'seq'))  229 us
    reduce_sum x6, other arithmetic, tap_sums(): rows_out.append(jnp.sum(jnp.where(same, signal * window, 0.0), axis=0))  38.3 us
    dot_general x12, matrix products, block_scores(): jnp.einsum('qhd,khd->hqk', query_blk, key_part, preferred_element_type=jn...  28.9 us
    all_to_all x1, waiting for transfers between devices, local(): lax.all_to_all(grad_k.reshape(total, -1), 'seq', split_axis=0, concat_axi...  15 us
    all_to_all x1, waiting for transfers between devices, local(): lax.all_to_all(key_proj[0], 'seq', split_axis=1, concat_axis=0, tiled=True)  14.6 us
    unnamed x114, local copies, waits for them, and re-layouts  12.8 us
  transfers between devices with their start and end apart: 11, of which 9 were waited for; matrix products, arithmetic and copies ran while one was open for 9% of the time, Pallas kernels for 0%

commit v1 on v0

--- a/solution.py
+++ b/solution.py
@@ -7,6 +7,11 @@
 HEAD_DIM = 64
 KERN = 31
 LAG = 30
+
+
+def move_the_region(a0):
+    opened = lax.psum(lax.psum(a0, axis_name="dp"), axis_name="seq")
+    return opened
 
 
 def shifted(value, axis, steps):
@@ -178,7 +183,7 @@
     weight_local = lax.dot_general(
         mixed_rows, proj_back, (((0,), (0,)), ((), ())), preferred_element_type=jnp.float32
     )
-    summed = lax.psum((weight_local, conv_local), ("dp", "seq"))
+    summed = move_the_region((weight_local, conv_local))
     weight_grad = summed[0] * factor
     conv_grad = summed[1] * factor
     mixed_back = lax.dot_general(

time: 615 us -> 494 us (0.80)
  waiting for transfers between devices: 314 us -> 184 us
  local copies, waits for them, and re-layouts: 68.6 us -> 75.4 us
  starting transfers between devices: 44.5 us -> 50.7 us
    psum x1 -> x2, waiting for transfers between devices: 229 us -> 104 us  [move_the_region(): opened = lax.psum(lax.psum(a0, axis_name='dp'), axis_name='seq')]
    unnamed x114 -> x66, local copies, waits for them, and re-layouts: 12.8 us -> 12.7 us
  transfers between devices with their start and end apart: 11 -> 12, of which waited for: 9 -> 9; matrix products, arithmetic and copies ran while one was open for 9% -> 27% of each run, Pallas kernels for 0% -> 0%
where the time goes in v1:
time: 494 us; the launch traced here: 490 us
  waiting for transfers between devices  184 us (37%)
  matrix products  83.5 us (17%)
  local copies, waits for them, and re-layouts  75.4 us (15%)
  other arithmetic  73.9 us (15%)
  starting transfers between devices  50.7 us (10%)
  between operations  14.6 us (3%)
  loops' own time  8.09 us (2%)
    psum x2, waiting for transfers between devices, move_the_region(): opened = lax.psum(lax.psum(a0, axis_name='dp'), axis_name='seq')  104 us
    reduce_sum x6, other arithmetic, tap_sums(): rows_out.append(jnp.sum(jnp.where(same, signal * window, 0.0), axis=0))  37.2 us
    dot_general x12, matrix products, block_scores(): jnp.einsum('qhd,khd->hqk', query_blk, key_part, preferred_element_type=jn...  28.9 us
    all_to_all x1, waiting for transfers between devices, local(): lax.all_to_all(key_proj[0], 'seq', split_axis=1, concat_axis=0, tiled=True)  15.9 us
    all_to_all x1, waiting for transfers between devices, local(): lax.all_to_all(grad_k.reshape(total, -1), 'seq', split_axis=0, concat_axi...  15.1 us
    all_to_all x1, waiting for transfers between devices, local(): lax.all_to_all(mixed_heads.reshape(total, -1), 'seq', split_axis=0, conca...  13.4 us
    unnamed x66, local copies, waits for them, and re-layouts  12.7 us
    all_to_all x1, waiting for transfers between devices, local(): lax.all_to_all(grad_v.reshape(total, -1), 'seq', split_axis=0, concat_axi...  12 us
  transfers between devices with their start and end apart: 12, of which 9 were waited for; matrix products, arithmetic and copies ran while one was open for 27% of the time, Pallas kernels for 0%

profile of v1, /device:TPU:2, one launch (start us, length us, event | category | flops | bytes accessed | tf_op | source)
XLA Modules:
  0.0 490.5 jit_solution(7153374393755855353)
XLA Ops:
  9.3 8.6 %all-to-all-start = ((bf16[192,16,64]{0,2,1:T(8,128)(2,1)}), bf16[192,16,64]{0,2,1:T(8,128)(2,1)S(1)}, u32[]{:S(2)}, u32[]{:S(2)}) async-start(bf16[192,16,64]{0,2,1:T(8,128)(2,1)} %bitcast.10), calls=%async_computation | async-start | bytes 1048576 | tf_op jit(solution)/shard_map/all_to_all | solution.py:148
  21.9 12.0 %all-to-all-done = bf16[192,16,64]{0,2,1:T(8,128)(2,1)S(1)} async-done(((bf16[192,16,64]{0,2,1:T(8,128)(2,1)}), bf16[192,16,64]{0,2,1:T(8,128)(2,1)S(1)}, u32[]{:S(2)}, u32[]{:S(2)}) %all-to-all-start) | async-done | bytes 393248 | tf_op jit(solution)/shard_map/all_to_all | solution.py:148
  33.9 4.2 all-to-all-start.1
  38.4 15.9 %all-to-all-done.1 = bf16[192,16,64]{0,2,1:T(8,128)(2,1)S(1)} async-done(((bf16[192,16,64]{0,2,1:T(8,128)(2,1)}), bf16[192,16,64]{0,2,1:T(8,128)(2,1)S(1)}, u32[]{:S(2)}, u32[]{:S(2)}) %all-to-all-start.1) | async-done | bytes 393248 | tf_op jit(solution)/shard_map/all_to_all | solution.py:149
  54.3 4.2 all-to-all-start.2
  64.1 10.5 %all-to-all-done.2 = bf16[192,16,64]{0,2,1:T(8,128)(2,1)} async-done(((bf16[192,16,64]{0,2,1:T(8,128)(2,1)}), bf16[192,16,64]{0,2,1:T(8,128)(2,1)}, u32[]{:S(2)}, u32[]{:S(2)}) %all-to-all-start.2) | async-done | bytes 393248 | tf_op jit(solution)/shard_map/all_to_all | solution.py:150
  76.6 41.2 %while.27 = (s32[]{:T(128)}, bf16[6,512,1,64]{1,3,2,0:T(8,128)(2,1)S(1)}, f32[6,1,512]{2,1,0:T(1,128)}, s32[6]{0:T(128)S(1)}, s32[3072]{0:T(1024)}, /*index=5*/b...) while((s32[]{:T(128)}, ...), condition=%wide.region_4.5_spmd, body=%wide.region_1.4_spmd.sunk | while | flops 415268352 | bytes 19828936 | solution.py:99
  123.3 4.1 all-to-all-start.3
  130.2 13.4 %all-to-all-done.3 = bf16[16,192,64]{1,2,0:T(8,128)(2,1)S(1)} async-done(((bf16[16,192,64]{1,2,0:T(8,128)(2,1)}), bf16[16,192,64]{1,2,0:T(8,128)(2,1)S(1)}, u32[]{:S(2)}, u32[]{:S(2)}) %all-to-all-start.3) | async-done | bytes 393248 | tf_op jit(solution)/shard_map/all_to_all | solution.py:157
  145.0 3.6 collective-permute-start
  152.0 19.7 %fusion.155 = (f32[1024]{0:T(1024)S(1)}, f32[192,1024]{1,0:T(8,128)S(1)}, f32[192,1024]{1,0:T(8,128)}) fusion(bf16[192,1024]{1,0:T(8,128)(2,1)} %copy-done.1, pred[192]{0:T(512)(128)(4,1)} %get-tuple-element.320, bf16[1,192,1024]{2,1,0:T(8,128)(2,1)} %param.14, f32[1024]{0:T(1024)} %bitcast.257, bf16[30,1024]{1,0:T(8,128)(2,1)S(1)} %collective-permute-done, ...), kind=kLoop, calls=%fused_computation.322 | loop fusion | flops 44235776 | bytes 2557760 | tf_op jit(solution)/shard_map/reduce_sum | solution.py:56
  173.0 4.1 fusion.90
  182.1 9.5 %fusion.151 = bf16[192,1024]{1,0:T(8,128)(2,1)S(1)} fusion(f32[192,1024]{1,0:T(8,128)S(1)} %get-tuple-element.252, f32[30,1024]{1,0:T(8,128)S(1)} %convert_element_type.251, bf16[1,192,1024]{2,1,0:T(8,128)(2,1)S(1)} %copy-done.13, f32[1024]{0:T(1024)} %bitcast.258, f32[1024]{0:T(1024)} %bitcast.260, f32[1024]{0:T(1024)} %bitcast.264, f32[1024]{0:T(1024)} %bitcast.266, ...), kind=kLoop, calls=%fused_computation.318 | loop fusion | flops 24576000 | bytes 1828672 | tf_op jit(solution)/shard_map/convert_element_type | solution.py:180
  196.0 6.2 %all-to-all-start.4 = ((bf16[192,16,64]{0,2,1:T(8,128)(2,1)}), bf16[192,16,64]{0,2,1:T(8,128)(2,1)}, u32[]{:S(2)}, u32[]{:S(2)}) async-start(bf16[192,16,64]{0,2,1:T(8,128)(2,1)} %bitcast.230), calls=%async_computation.4 | async-start | bytes 1048576 | tf_op jit(solution)/shard_map/all_to_all | solution.py:192
  202.5 4.2 fusion.126
  206.7 4.2 fusion.150
  213.6 3.9 fusion.313
  223.6 80.9 %while.28 = (s32[]{:T(128)}, f32[3072,1,64]{0,2,1:T(8,128)}, f32[3072,1,64]{0,2,1:T(8,128)S(1)}, bf16[6,512,1,64]{1,3,2,0:T(8,128)(2,1)}, s32[6]{0:T(128)S(1)}, ...) while((s32[]{:T(128)}, f32[3072,1,64]{0,2,1:T(8,128)}, ...), condition=%wide.region_10.11_spmd.clone, body=%wide.region_8.10_spmd.clone.sunk | while | flops 1021967872 | bytes 31551828 | solution.py:132
  226.5 2.7 exponential_convert_fusion.12
  240.0 2.7 exponential_convert_fusion.12
  253.5 2.7 exponential_convert_fusion.12
  267.0 2.7 exponential_convert_fusion.12
  280.5 2.7 exponential_convert_fusion.12
  293.9 2.7 exponential_convert_fusion.12
  311.0 6.5 %all-to-all-start.5 = ((bf16[16,192,64]{1,2,0:T(8,128)(2,1)}), bf16[16,192,64]{1,2,0:T(8,128)(2,1)}, u32[]{:S(2)}, u32[]{:S(2)}) async-start(bf16[16,192,64]{1,2,0:T(8,128)(2,1)} %copy.68), calls=%async_computation.5 | async-start | bytes 1048576 | tf_op jit(solution)/shard_map/all_to_all | solution.py:199
  317.6 16.7 %all-reduce.7.cloned.1.call-done = (f32[1024,1024]{1,0:T(8,128)}, f32[31,1024]{1,0:T(8,128)}) async-done(((f32[1024,1024]{1,0:T(8,128)}, f32[31,1024]{1,0:T(8,128)}), (f32[1024,1024]{1,0:T(8,128)}, f32[31,1024]{1,0:T(8,128)})) %all-reduce.7.cloned.1.call-update) | async-done | bytes 4321296 | tf_op jit(solution)/shard_map/psum | solution.py:13
  340.7 7.2 %all-to-all-start.6 = ((bf16[16,192,64]{1,2,0:T(8,128)(2,1)}), bf16[16,192,64]{1,2,0:T(8,128)(2,1)}, u32[]{:S(2)}, u32[]{:S(2)}) async-start(bf16[16,192,64]{1,2,0:T(8,128)(2,1)} %copy.69), calls=%async_computation.6 | async-start | bytes 1048576 | tf_op jit(solution)/shard_map/all_to_all | solution.py:200
  351.3 15.1 %all-to-all-done.6 = bf16[16,192,64]{1,2,0:T(8,128)(2,1)} async-done(((bf16[16,192,64]{1,2,0:T(8,128)(2,1)}), bf16[16,192,64]{1,2,0:T(8,128)(2,1)}, u32[]{:S(2)}, u32[]{:S(2)}) %all-to-all-start.6) | async-done | bytes 393248 | tf_op jit(solution)/shard_map/all_to_all | solution.py:200
  366.4 4.6 all-to-all-start.7
  377.1 12.0 %all-to-all-done.7 = bf16[16,192,64]{1,2,0:T(8,128)(2,1)S(1)} async-done(((bf16[16,192,64]{1,2,0:T(8,128)(2,1)}), bf16[16,192,64]{1,2,0:T(8,128)(2,1)S(1)}, u32[]{:S(2)}, u32[]{:S(2)}) %all-to-all-start.7) | async-done | bytes 393248 | tf_op jit(solution)/shard_map/all_to_all | solution.py:201
  390.1 87.8 %all-reduce.5.cloned.1.call-done = (f32[1024,1024]{1,0:T(8,128)}, f32[31,1024]{1,0:T(8,128)}) async-done(((f32[1024,1024]{1,0:T(8,128)}, f32[31,1024]{1,0:T(8,128)}), (f32[1024,1024]{1,0:T(8,128)}, f32[31,1024]{1,0:T(8,128)})) %all-reduce.5.cloned.1.call-update) | async-done | bytes 4321296 | tf_op jit(solution)/shard_map/psum | solution.py:13
  477.8 5.2 %broadcast_multiply_fusion = f32[1024,1024]{1,0:T(8,128)} fusion(f32[1024,1024]{1,0:T(8,128)} %get-tuple-element.247), kind=kLoop, calls=%fused_computation.101 | loop fusion | flops 1048576 | bytes 8388608 | tf_op jit(solution)/shard_map/mul | solution.py:187
  (255 shorter events, 167.9 us)
Async XLA Ops:
  7.2 136.4 %copy-start = (bf16[1024,1024]{1,0:T(8,128)(2,1)S(1)}, bf16[1024,1024]{1,0:T(8,128)(2,1)}, u32[]{:S(2)}) copy-start(bf16[1024,1024]{1,0:T(8,128)(2,1)} %param.15) | copy-start | bytes 6291460
  7.2 31.0 %copy-start.20 = (s32[1,2]{1,0:T(1,128)S(1)}, s32[1,2]{1,0:T(1,128)}, u32[]{:S(2)}) copy-start(s32[1,2]{1,0:T(1,128)} %param.17) | copy-start | bytes 28
  9.3 24.6 %all-to-all-start = ((bf16[192,16,64]{0,2,1:T(8,128)(2,1)}), bf16[192,16,64]{0,2,1:T(8,128)(2,1)S(1)}, u32[]{:S(2)}, u32[]{:S(2)}) async-start(bf16[192,16,64]{0,2,1:T(8,128)(2,1)} %bitcast.10), calls=%async_computation | async-start | bytes 1048576 | tf_op jit(solution)/shard_map/all_to_all | solution.py:148
  33.9 20.4 %all-to-all-start.1 = ((bf16[192,16,64]{0,2,1:T(8,128)(2,1)}), bf16[192,16,64]{0,2,1:T(8,128)(2,1)S(1)}, u32[]{:S(2)}, u32[]{:S(2)}) async-start(bf16[192,16,64]{0,2,1:T(8,128)(2,1)} %bitcast.12), calls=%async_computation.1 | async-start | bytes 1048576 | tf_op jit(solution)/shard_map/all_to_all | solution.py:149
  54.3 20.3 %all-to-all-start.2 = ((bf16[192,16,64]{0,2,1:T(8,128)(2,1)}), bf16[192,16,64]{0,2,1:T(8,128)(2,1)}, u32[]{:S(2)}, u32[]{:S(2)}) async-start(bf16[192,16,64]{0,2,1:T(8,128)(2,1)} %bitcast.14), calls=%async_computation.2 | async-start | bytes 1048576 | tf_op jit(solution)/shard_map/all_to_all | solution.py:150
  59.3 68.9 %copy-start.17 = (s32[192]{0:T(256)}, s32[192]{0:T(256)S(1)}, u32[]{:S(2)}) copy-start(s32[192]{0:T(256)S(1)} %get-tuple-element.255) | copy-start | bytes 2308
  76.6 52.3 %copy-start.15 = (f32[31,1024]{1,0:T(8,128)S(1)}, f32[31,1024]{1,0:T(8,128)}, u32[]{:S(2)}) copy-start(f32[31,1024]{1,0:T(8,128)} %param.16) | copy-start | bytes 380932
  117.8 34.2 %copy-start.7 = (bf16[3072,1,64]{0,2,1:T(8,128)(2,1)}, bf16[3072,1,64]{0,2,1:T(8,128)(2,1)S(1)}, u32[]{:S(2)}) copy-start(bf16[3072,1,64]{0,2,1:T(8,128)(2,1)S(1)} %get-tuple-element.573) | copy-start | bytes 1179652
  123.3 20.3 %all-to-all-start.3 = ((bf16[16,192,64]{1,2,0:T(8,128)(2,1)}), bf16[16,192,64]{1,2,0:T(8,128)(2,1)S(1)}, u32[]{:S(2)}, u32[]{:S(2)}) async-start(bf16[16,192,64]{1,2,0:T(8,128)(2,1)} %copy.63), calls=%async_computation.3 | async-start | bytes 1048576 | tf_op jit(solution)/shard_map/all_to_all | solution.py:157
  145.0 7.0 %collective-permute-start = (bf16[30,1024]{1,0:T(8,128)(2,1)S(1)}, bf16[30,1024]{1,0:T(8,128)(2,1)S(1)}, u32[]{:S(2)}, u32[]{:S(2)}) collective-permute-start(bf16[30,1024]{1,0:T(8,128)(2,1)S(1)} %slice.713), channel_id=1, source_target_pairs={{0,1},{1,2},{2,3},{3,4},{4,5},{5,6},{6,7},{7,8},{8,9},{9,10},{10,1... | collective-permute-start | bytes 184328 | tf_op jit(solution)/shard_map/ppermute | solution.py:20
  150.0 27.3 %copy-start.2 = (bf16[192,1024]{1,0:T(8,128)(2,1)S(1)}, bf16[192,1024]{1,0:T(8,128)(2,1)}, u32[]{:S(2)}) copy-start(bf16[192,1024]{1,0:T(8,128)(2,1)} %copy-done.1) | copy-start | bytes 1179652
  150.0 32.1 %copy-start.13 = (bf16[1,192,1024]{2,1,0:T(8,128)(2,1)S(1)}, bf16[1,192,1024]{2,1,0:T(8,128)(2,1)}, u32[]{:S(2)}) copy-start(bf16[1,192,1024]{2,1,0:T(8,128)(2,1)} %param.14) | copy-start | bytes 1179652
  150.0 32.0 %copy-start.21 = (pred[192]{0:T(512)(128)(4,1)S(1)}, pred[192]{0:T(512)(128)(4,1)}, u32[]{:S(2)}) copy-start(pred[192]{0:T(512)(128)(4,1)} %get-tuple-element.307) | copy-start | bytes 580
  150.0 32.0 %copy-start.22 = (pred[192]{0:T(512)(128)(4,1)S(1)}, pred[192]{0:T(512)(128)(4,1)}, u32[]{:S(2)}) copy-start(pred[192]{0:T(512)(128)(4,1)} %get-tuple-element.308) | copy-start | bytes 580
  150.0 32.0 %copy-start.23 = (pred[192]{0:T(512)(128)(4,1)S(1)}, pred[192]{0:T(512)(128)(4,1)}, u32[]{:S(2)}) copy-start(pred[192]{0:T(512)(128)(4,1)} %get-tuple-element.309) | copy-start | bytes 580
  150.0 32.0 %copy-start.24 = (pred[192]{0:T(512)(128)(4,1)S(1)}, pred[192]{0:T(512)(128)(4,1)}, u32[]{:S(2)}) copy-start(pred[192]{0:T(512)(128)(4,1)} %get-tuple-element.310) | copy-start | bytes 580
  150.0 32.0 %copy-start.25 = (pred[192]{0:T(512)(128)(4,1)S(1)}, pred[192]{0:T(512)(128)(4,1)}, u32[]{:S(2)}) copy-start(pred[192]{0:T(512)(128)(4,1)} %get-tuple-element.311) | copy-start | bytes 580
  150.0 32.0 %copy-start.26 = (pred[192]{0:T(512)(128)(4,1)S(1)}, pred[192]{0:T(512)(128)(4,1)}, u32[]{:S(2)}) copy-start(pred[192]{0:T(512)(128)(4,1)} %get-tuple-element.312) | copy-start | bytes 580
  150.0 32.0 %copy-start.27 = (pred[192]{0:T(512)(128)(4,1)S(1)}, pred[192]{0:T(512)(128)(4,1)}, u32[]{:S(2)}) copy-start(pred[192]{0:T(512)(128)(4,1)} %get-tuple-element.313) | copy-start | bytes 580
  150.0 32.0 %copy-start.28 = (pred[192]{0:T(512)(128)(4,1)S(1)}, pred[192]{0:T(512)(128)(4,1)}, u32[]{:S(2)}) copy-start(pred[192]{0:T(512)(128)(4,1)} %get-tuple-element.314) | copy-start | bytes 580
  150.1 32.0 %copy-start.29 = (pred[192]{0:T(512)(128)(4,1)S(1)}, pred[192]{0:T(512)(128)(4,1)}, u32[]{:S(2)}) copy-start(pred[192]{0:T(512)(128)(4,1)} %get-tuple-element.315) | copy-start | bytes 580
  150.1 32.0 %copy-start.30 = (pred[192]{0:T(512)(128)(4,1)S(1)}, pred[192]{0:T(512)(128)(4,1)}, u32[]{:S(2)}) copy-start(pred[192]{0:T(512)(128)(4,1)} %get-tuple-element.316) | copy-start | bytes 580
  150.1 32.0 %copy-start.31 = (pred[192]{0:T(512)(128)(4,1)S(1)}, pred[192]{0:T(512)(128)(4,1)}, u32[]{:S(2)}) copy-start(pred[192]{0:T(512)(128)(4,1)} %get-tuple-element.317) | copy-start | bytes 580
  150.1 32.0 %copy-start.32 = (pred[192]{0:T(512)(128)(4,1)S(1)}, pred[192]{0:T(512)(128)(4,1)}, u32[]{:S(2)}) copy-start(pred[192]{0:T(512)(128)(4,1)} %get-tuple-element.318) | copy-start | bytes 580
  171.7 10.3 %collective-permute-start.1 = (bf16[30,1024]{1,0:T(8,128)(2,1)S(1)}, bf16[30,1024]{1,0:T(8,128)(2,1)S(1)}, u32[]{:S(2)}, u32[]{:S(2)}) collective-permute-start(bf16[30,1024]{1,0:T(8,128)(2,1)S(1)} %slice.1694), channel_id=1, source_target_pairs={{1,0},{2,1},{3,2},{4,3},{5,4},{6,5},{7,6},{8,7},{9,8},{10,9},{11,1... | collective-permute-start | bytes 184328 | tf_op jit(solution)/shard_map/ppermute | solution.py:20
  196.0 22.2 %all-to-all-start.4 = ((bf16[192,16,64]{0,2,1:T(8,128)(2,1)}), bf16[192,16,64]{0,2,1:T(8,128)(2,1)}, u32[]{:S(2)}, u32[]{:S(2)}) async-start(bf16[192,16,64]{0,2,1:T(8,128)(2,1)} %bitcast.230), calls=%async_computation.4 | async-start | bytes 1048576 | tf_op jit(solution)/shard_map/all_to_all | solution.py:192
  202.2 132.1 %all-reduce.7.cloned.1.call-start = ((), (), s32[]{:S(2)}) async-start(), calls=%async_computation.9 | async-start | bytes 8650752 | tf_op jit(solution)/shard_map/psum | solution.py:13
  311.0 29.7 %all-to-all-start.5 = ((bf16[16,192,64]{1,2,0:T(8,128)(2,1)}), bf16[16,192,64]{1,2,0:T(8,128)(2,1)}, u32[]{:S(2)}, u32[]{:S(2)}) async-start(bf16[16,192,64]{1,2,0:T(8,128)(2,1)} %copy.68), calls=%async_computation.5 | async-start | bytes 1048576 | tf_op jit(solution)/shard_map/all_to_all | solution.py:199
  317.5 160.3 %all-reduce.5.cloned.1.call-start = ((), (), s32[]{:S(2)}) async-start(), calls=%async_computation.8 | async-start | bytes 8650752 | tf_op jit(solution)/shard_map/psum | solution.py:13
  334.3 36.7 %copy-start.3 = (bf16[192,1024]{1,0:T(8,128)(2,1)S(1)}, bf16[192,1024]{1,0:T(8,128)(2,1)}, u32[]{:S(2)}) copy-start(bf16[192,1024]{1,0:T(8,128)(2,1)} %copy-done.1) | copy-start | bytes 1179652
  340.7 25.6 %all-to-all-start.6 = ((bf16[16,192,64]{1,2,0:T(8,128)(2,1)}), bf16[16,192,64]{1,2,0:T(8,128)(2,1)}, u32[]{:S(2)}, u32[]{:S(2)}) async-start(bf16[16,192,64]{1,2,0:T(8,128)(2,1)} %copy.69), calls=%async_computation.6 | async-start | bytes 1048576 | tf_op jit(solution)/shard_map/all_to_all | solution.py:200
  366.4 22.7 %all-to-all-start.7 = ((bf16[16,192,64]{1,2,0:T(8,128)(2,1)}), bf16[16,192,64]{1,2,0:T(8,128)(2,1)S(1)}, u32[]{:S(2)}, u32[]{:S(2)}) async-start(bf16[16,192,64]{1,2,0:T(8,128)(2,1)} %copy.70), calls=%async_computation.7 | async-start | bytes 1048576 | tf_op jit(solution)/shard_map/all_to_all | solution.py:201
  (28 other events, 115.8 us)
Sparse Core Ops, SparseCore 0:
  217.7 116.5 all-reduce.6
  336.9 140.8 all-reduce.4
